TPU v7x, 128 devices: a whole 4x4x4 slice. The times are simulated.
128 devices in a mesh: row: 8 (over x, core), col: 16 (over y, z).
Axes of the slice: x: 4, y: 4, z: 4, core: 2. Of those that a mesh axis runs over, the one named last changes fastest.
Arguments:
- trail: bfloat16 [16384, 16384], P('row', 'col'), may hold values from -0.046875 to 0.046875
- row_one: bfloat16 [128, 16384], P('row', 'col'), may hold values from -0.5 to 0.5
- row_two: bfloat16 [128, 16384], P('row', 'col'), may hold values from -0.5 to 0.5
- diag_one: float32 [128, 128], replicated, may hold values from -1 to 2, as said below
- diag_two: float32 [128, 128], replicated, may hold values from -1 to 2, as said below
- adj_trail: float32 [16384, 16384], P('row', 'col'), may hold values from -6 to 6
- adj_row_one: float32 [128, 16384], P('row', 'col'), may hold values from -6 to 6
- adj_row_two: float32 [128, 16384], P('row', 'col'), may hold values from -6 to 6
- adj_diag_one: float32 [128, 128], replicated, may hold values from -6 to 6
- adj_diag_two: float32 [128, 128], replicated, may hold values from -6 to 6
Outputs:
- grad_trail: bfloat16 [16384, 16384], P('row', 'col')
- grad_row_one: float32 [128, 16384], P('row', 'col')
- grad_row_two: float32 [128, 16384], P('row', 'col')
- grad_diag_one: float32 [128, 128], replicated
- grad_diag_two: float32 [128, 128], replicated
Inputs may be any that keep to these rules, and one draw needn't show every extreme that they name: `diag_one`: lower triangular with a positive diagonal. `diag_two`: lower triangular with a positive diagonal.
All inputs are finite; a program needn't handle non-finite values.
Results may differ from a plain program's by a relative error of at most 0.014.
Values may be sent and summed in bfloat16 or wider, within the bound.
A program may use at most 128 MiB of HBM per device.

v0:
```python
import jax
import jax.numpy as jnp
from jax import lax
from jax.sharding import PartitionSpec as P

exact_mode = lax.Precision.HIGHEST


def from_root(value, axis, source):
    kept = jnp.where(lax.axis_index(axis) == source, value, 0).astype(value.dtype)
    return lax.psum(kept, axis)


def halved_lower(matrix):
    order = matrix.shape[0]
    keep = jnp.tril(jnp.ones((order, order), matrix.dtype)) - 0.5 * jnp.eye(
        order, dtype=matrix.dtype
    )
    return matrix * keep


def inverse_lower(block):
    ident = jnp.eye(block.shape[0], dtype=block.dtype)
    return lax.linalg.triangular_solve(block, ident, left_side=True, lower=True)


def block_adjoint(block, inverse, seed_adj):
    inner = halved_lower(jnp.dot(block.T, seed_adj, precision=exact_mode))
    middle = jnp.dot(inverse.T, inner, precision=exact_mode)
    return halved_lower(jnp.dot(middle, inverse, precision=exact_mode))


def per_device(
    trail,
    row_one,
    row_two,
    diag_one,
    diag_two,
    adj_trail,
    adj_row_one,
    adj_row_two,
    adj_diag_one,
    adj_diag_two,
):
    panel = diag_one.shape[0]
    width = trail.shape[1]
    band = row_one.shape[0]
    last = width - panel
    col_count = lax.axis_size("col")
    col_here = lax.axis_index("col")
    row_start = lax.axis_index("row") * band
    here_one = col_here == col_count - 2
    here_two = col_here == col_count - 1
    full_one, full_two = (
        lax.all_gather(row_one, "row", axis=0, tiled=True),
        lax.all_gather(row_two, "row", axis=0, tiled=True),
    )

    def own_rows(matrix):
        return lax.dynamic_slice_in_dim(matrix, row_start, band, 0)

    def solve_panel(rows, inverse, root):
        whole = from_root(rows, "col", root)
        return jnp.dot(whole, inverse, precision=exact_mode).astype(jnp.bfloat16)

    def summed_block(partial_value, root):
        rows_sum = lax.psum(partial_value, "row")
        return from_root(rows_sum, "col", root)

    inverse_two = inverse_lower(diag_two)
    solved_two = solve_panel(adj_trail[:, last:], inverse_two, col_count - 1)
    partial_two = jnp.dot(solved_two.T, trail[:, last:], preferred_element_type=jnp.float32)
    seed_two = jnp.tril(adj_diag_two - summed_block(partial_two, col_count - 1))
    grad_diag_two = block_adjoint(diag_two, inverse_two, seed_two)
    mirror_two = own_rows(grad_diag_two + grad_diag_two.T)
    rest_two = jnp.dot(mirror_two, full_two.astype(jnp.float32), precision=exact_mode)
    inverse_one = inverse_lower(diag_one)
    crossed = lax.psum_scatter(
        jnp.dot(solved_two.T, trail, preferred_element_type=jnp.float32).astype(jnp.bfloat16),
        "row",
        scatter_dimension=0,
        tiled=True,
    ).astype(jnp.float32)
    adj_two = adj_row_two - crossed - rest_two
    adj_next = adj_trail - jnp.dot(solved_two, full_two, preferred_element_type=jnp.float32)
    stacked = jnp.concatenate([adj_two[:, last:], adj_next[:, last:]], 0)
    solved_one = solve_panel(stacked, inverse_one, col_count - 2)
    head_rows = solved_one[:band]
    tail_rows = solved_one[band:]
    partial_one = jnp.dot(
        head_rows.T, row_two[:, last:], preferred_element_type=jnp.float32
    ) + jnp.dot(tail_rows.T, trail[:, last:], preferred_element_type=jnp.float32)
    seed_one = jnp.tril(adj_diag_one - summed_block(partial_one, col_count - 2))
    grad_diag_one = block_adjoint(diag_one, inverse_one, seed_one)
    mirror_one = own_rows(grad_diag_one + grad_diag_one.T)
    rest_one = jnp.dot(mirror_one, full_one.astype(jnp.float32), precision=exact_mode)
    head_update = jnp.dot(head_rows, full_one, preferred_element_type=jnp.float32)
    two_left = adj_two - head_update
    trail_left = adj_next - jnp.dot(tail_rows, full_one, preferred_element_type=jnp.float32)
    crossed_one = lax.psum_scatter(
        (
            jnp.dot(head_rows.T, row_two, preferred_element_type=jnp.float32)
            + jnp.dot(tail_rows.T, trail, preferred_element_type=jnp.float32)
        ).astype(jnp.bfloat16),
        "row",
        scatter_dimension=0,
        tiled=True,
    ).astype(jnp.float32)
    one_left = adj_row_one - crossed_one - rest_one
    trail_block = jnp.where(
        here_one,
        tail_rows.astype(jnp.float32),
        jnp.where(here_two, solved_two.astype(jnp.float32), trail_left[:, last:]),
    )
    grad_trail = jnp.concatenate([trail_left[:, :last], trail_block], 1).astype(jnp.bfloat16)
    zero_block = jnp.zeros((band, panel), jnp.float32)
    one_block = jnp.where(here_one | here_two, zero_block, one_left[:, last:])
    grad_row_one = jnp.concatenate([one_left[:, :last], one_block], 1)
    two_block = jnp.where(
        here_one, head_rows.astype(jnp.float32), jnp.where(here_two, zero_block, two_left[:, last:])
    )
    grad_row_two = jnp.concatenate([two_left[:, :last], two_block], 1)
    return (grad_trail, grad_row_one, grad_row_two, grad_diag_one, grad_diag_two)


def solution(mesh):
    in_specs = (
        P("row", "col"),
        P("row", "col"),
        P("row", "col"),
        P(),
        P(),
        P("row", "col"),
        P("row", "col"),
        P("row", "col"),
        P(),
        P(),
    )
    out_specs = (P("row", "col"), P("row", "col"), P("row", "col"), P(), P())
    return jax.shard_map(
        per_device, mesh=mesh, in_specs=in_specs, out_specs=out_specs, check_vma=False
    )
```

profile of v0, /device:TPU:0, one launch (start us, length us, event | category | flops | bytes accessed | tf_op | source)
XLA Modules:
  0.0 564.0 jit_solution(18032866646956129577)
XLA Ops:
  7.2 2.3 slice_select_fusion.1
  9.6 0.9 select_bitcast_fusion.1
  10.4 9.8 %custom-call.4 = f32[1,128,128]{1,2,0:T(8,128)S(1)} custom-call(f32[1,128,128]{2,1,0:T(8,128)S(1)} %select_bitcast_fusion.1), custom_call_target="InvertDiagBlocksLowerTriangular" | custom-call | tf_op jit(solution)/shard_map/triangular_solve/custom-call.1 | solution.py:24
  20.3 13.5 %all_gather.6 = bf16[128,1024]{1,0:T(8,128)(2,1)S(1)} all-gather(bf16[16,1024]{1,0:T(8,128)(2,1)} %param.14), channel_id=1, replica_groups=mesh['row'=8,'col'=16] {'row'}, dimensions={0}, use_global_device_ids=true | all-gather | bytes 294912 | tf_op jit(solution)/shard_map/all_gather | solution.py:56
  34.0 67.5 %all-reduce.7.cloned.1.call-done = f32[2048,128]{1,0:T(8,128)} async-done(((f32[2048,128]{1,0:T(8,128)}), f32[2048,128]{1,0:T(8,128)}) %all-reduce.7.cloned.1.call-update) | async-done | bytes 1048592 | tf_op jit(solution)/shard_map/psum | solution.py:11
  101.5 2.2 convolution_convert_fusion.1
  103.7 2.0 fusion.6
  105.8 7.9 %convolution_subtract_fusion.1 = f32[2048,1024]{1,0:T(8,128)} fusion(f32[2048,1024]{1,0:T(8,128)} %param.17, bf16[2048,128]{1,0:T(8,128)(2,1)S(1)} %convolution_convert_fusion.1, bf16[128,1024]{1,0:T(8,128)(2,1)S(1)} %all_gather.6), kind=kOutput, calls=%fused_computation.2 | convolution fusion | flops 538968064 | bytes 17563648 | tf_op jit(solution)/shard_map/dot_general | solution.py:85
  113.6 50.0 %all-reduce.9.cloned.1.call-done = f32[128,128]{1,0:T(8,128)} async-done(((f32[128,128]{1,0:T(8,128)}), f32[128,128]{1,0:T(8,128)}) %all-reduce.9.cloned.1.call-update) | async-done | bytes 65552 | tf_op jit(solution)/shard_map/psum | solution.py:67
  163.6 0.6 broadcast_select_fusion.1
  164.3 3.7 convolution_convert_fusion.2
  168.1 79.6 %all-reduce.11.cloned.1.call-done = f32[128,128]{1,0:T(8,128)} async-done(((f32[128,128]{1,0:T(8,128)}), f32[128,128]{1,0:T(8,128)}) %all-reduce.11.cloned.1.call-update) | async-done | bytes 65552 | tf_op jit(solution)/shard_map/psum | solution.py:11
  247.7 1.1 fusion.2
  249.5 30.7 %reduce-scatter.7.cloned.1.call-done = bf16[16,1024]{1,0:T(8,128)(2,1)} async-done(((bf16[128,1024]{1,0:T(8,128)(2,1)}), bf16[16,1024]{1,0:T(8,128)(2,1)}) %reduce-scatter.7.cloned.1.call-update) | async-done | bytes 32784 | tf_op jit(solution)/shard_map/reduce_scatter | solution.py:78
  280.2 1.0 convolution_subtract_fusion.4
  281.2 1.0 maximum_select_fusion
  282.4 9.8 %custom-call.5 = f32[1,128,128]{1,2,0:T(8,128)S(1)} custom-call(f32[1,128,128]{2,1,0:T(8,128)S(1)} %select_bitcast_fusion), custom_call_target="InvertDiagBlocksLowerTriangular" | custom-call | tf_op jit(solution)/shard_map/triangular_solve/custom-call.1 | solution.py:24
  292.2 13.0 %all_gather.7 = bf16[128,1024]{1,0:T(8,128)(2,1)S(1)} all-gather(bf16[16,1024]{1,0:T(8,128)(2,1)S(1)} %copy-done.10), channel_id=1, replica_groups=mesh['row'=8,'col'=16] {'row'}, dimensions={0}, use_global_device_ids=true | all-gather | bytes 294912 | tf_op jit(solution)/shard_map/all_gather | solution.py:55
  305.5 64.7 %all-reduce.13.cloned.1.call-done = f32[2064,128]{1,0:T(8,128)} async-done(((f32[2064,128]{1,0:T(8,128)}), f32[2064,128]{1,0:T(8,128)}) %all-reduce.13.cloned.1.call-update) | async-done | bytes 1056784 | tf_op jit(solution)/shard_map/psum | solution.py:11
  370.2 2.2 convolution_convert_fusion
  373.0 6.7 %convolution_subtract_fusion = bf16[2048,1024]{1,0:T(8,128)(2,1)} fusion(f32[2048,1024]{1,0:T(8,128)} %convolution_subtract_fusion.1, bf16[128,1024]{1,0:T(8,128)(2,1)S(1)} %all_gather.7, bf16[2064,128]{1,0:T(8,128)(2,1)S(1)} %convolution_convert_fusion), kind=kOutput, calls=%fused_computation.1 | convolution fusion | flops 541065216 | bytes 13369344 | tf_op jit(solution)/shard_map/dot_general | solution.py:99
  379.7 2.0 convolution_add_fusion.1
  381.7 3.6 fusion
  385.4 1.2 fusion.4
  386.7 4.1 slice.97
  390.8 48.5 %all-reduce.15.cloned.1.call-done = f32[128,128]{1,0:T(8,128)} async-done(((f32[128,128]{1,0:T(8,128)}), f32[128,128]{1,0:T(8,128)}) %all-reduce.15.cloned.1.call-update) | async-done | bytes 65552 | tf_op jit(solution)/shard_map/psum | solution.py:67
  439.3 0.6 broadcast_select_fusion
  440.7 4.7 pad_maximum_fusion
  445.4 78.0 %all-reduce.17.cloned.1.call-done = f32[128,128]{1,0:T(8,128)} async-done(((f32[128,128]{1,0:T(8,128)}), f32[128,128]{1,0:T(8,128)}) %all-reduce.17.cloned.1.call-update) | async-done | bytes 65552 | tf_op jit(solution)/shard_map/psum | solution.py:11
  523.4 1.1 fusion.1
  525.2 30.3 %reduce-scatter.9.cloned.1.call-done = bf16[16,1024]{1,0:T(8,128)(2,1)} async-done(((bf16[128,1024]{1,0:T(8,128)(2,1)}), bf16[16,1024]{1,0:T(8,128)(2,1)}) %reduce-scatter.9.cloned.1.call-update) | async-done | bytes 32784 | tf_op jit(solution)/shard_map/reduce_scatter | solution.py:100
  555.5 1.0 convolution_subtract_fusion.3
  (61 shorter events, 4.2 us)
Async XLA Ops:
  7.2 94.3 %all-reduce.7.cloned.1.call-start = ((), (), s32[]{:S(2)}) async-start(), calls=%async_computation.2 | async-start | bytes 2097152 | tf_op jit(solution)/shard_map/psum | solution.py:11
  9.5 154.1 %all-reduce.9.cloned.1.call-start = ((), (), s32[]{:S(2)}) async-start(), calls=%async_computation.3 | async-start | bytes 131072 | tf_op jit(solution)/shard_map/psum | solution.py:67
  105.7 142.0 %all-reduce.11.cloned.1.call-start = ((), (), s32[]{:S(2)}) async-start(), calls=%async_computation.4 | async-start | bytes 131072 | tf_op jit(solution)/shard_map/psum | solution.py:11
  113.6 134.1 %copy-start.1 = (f32[128,128]{1,0:T(8,128)S(1)}, f32[128,128]{1,0:T(8,128)}, u32[]{:S(2)}) copy-start(f32[128,128]{1,0:T(8,128)} %param.16) | copy-start | bytes 196612
  113.6 134.1 %copy-start.6 = (f32[128,128]{1,0:T(8,128)S(1)}, f32[128,128]{1,0:T(8,128)}, u32[]{:S(2)}) copy-start(f32[128,128]{1,0:T(8,128)} %param.21) | copy-start | bytes 196612
  113.6 166.6 %copy-start.7 = (f32[16,1024]{1,0:T(8,128)S(1)}, f32[16,1024]{1,0:T(8,128)}, u32[]{:S(2)}) copy-start(f32[16,1024]{1,0:T(8,128)} %param.19) | copy-start | bytes 196612
  164.3 117.0 %slice-start = ((f32[2048,1024]{1,0:T(8,128)}), f32[2048,128]{1,0:T(8,128)S(1)}, s32[]{:S(2)}) async-start(f32[2048,1024]{1,0:T(8,128)} %convolution_subtract_fusion.1), calls=%async_computation.10 | async-start | bytes 2097152 | tf_op jit(solution)/shard_map/slice | solution.py:86
  164.3 116.0 %reduce-scatter.7.cloned.1.call-start = ((), (), s32[]{:S(2)}) async-start(), calls=%async_computation.8 | async-start | bytes 294912 | tf_op jit(solution)/shard_map/reduce_scatter | solution.py:78
  168.0 114.3 %copy-start.2 = (f32[128,128]{1,0:T(8,128)S(1)}, f32[128,128]{1,0:T(8,128)}, u32[]{:S(2)}) copy-start(f32[128,128]{1,0:T(8,128)} %param.15) | copy-start | bytes 196612
  168.0 124.2 %copy-start.10 = (bf16[16,1024]{1,0:T(8,128)(2,1)S(1)}, bf16[16,1024]{1,0:T(8,128)(2,1)}, u32[]{:S(2)}) copy-start(bf16[16,1024]{1,0:T(8,128)(2,1)} %param.13) | copy-start | bytes 98308
  168.0 204.4 %copy-start.3 = (bf16[16,1024]{1,0:T(8,128)(2,1)S(1)}, bf16[16,1024]{1,0:T(8,128)(2,1)}, u32[]{:S(2)}) copy-start(bf16[16,1024]{1,0:T(8,128)(2,1)} %param.14) | copy-start | bytes 98308
  168.1 202.1 %all-reduce.13.cloned.1.call-start = ((), (), s32[]{:S(2)}) async-start(), calls=%async_computation.5 | async-start | bytes 2113536 | tf_op jit(solution)/shard_map/psum | solution.py:11
  249.4 130.3 %copy-start.4 = (f32[128,128]{1,0:T(8,128)}, f32[128,128]{1,0:T(8,128)S(1)}, u32[]{:S(2)}) copy-start(f32[128,128]{1,0:T(8,128)S(1)} %get-tuple-element.16) | copy-start | bytes 196612
  282.3 157.0 %all-reduce.15.cloned.1.call-start = ((), (), s32[]{:S(2)}) async-start(), calls=%async_computation.6 | async-start | bytes 131072 | tf_op jit(solution)/shard_map/psum | solution.py:67
  373.0 13.7 %copy-start = (f32[16,1024]{1,0:T(8,128)}, f32[16,1024]{1,0:T(8,128)S(1)}, u32[]{:S(2)}) copy-start(f32[16,1024]{1,0:T(8,128)S(1)} %convolution_subtract_fusion.2) | copy-start | bytes 196612
  381.7 141.7 %all-reduce.17.cloned.1.call-start = ((), (), s32[]{:S(2)}) async-start(), calls=%async_computation.7 | async-start | bytes 131072 | tf_op jit(solution)/shard_map/psum | solution.py:11
  386.6 53.4 %slice-start.1 = ((f32[16,1024]{1,0:T(8,128)}), f32[16,896]{1,0:T(8,128)S(1)}, s32[]{:S(2)}) async-start(f32[16,1024]{1,0:T(8,128)} %copy-done), calls=%async_computation.11 | async-start | bytes 114688 | tf_op jit(solution)/shard_map/slice | solution.py:122
  440.0 115.5 %reduce-scatter.9.cloned.1.call-start = ((), (), s32[]{:S(2)}) async-start(), calls=%async_computation.9 | async-start | bytes 294912 | tf_op jit(solution)/shard_map/reduce_scatter | solution.py:100
  440.7 82.7 %copy-start.8 = (f32[128,128]{1,0:T(8,128)S(1)}, f32[128,128]{1,0:T(8,128)}, u32[]{:S(2)}) copy-start(f32[128,128]{1,0:T(8,128)} %param.20) | copy-start | bytes 196612
  440.7 114.8 %copy-start.9 = (f32[16,1024]{1,0:T(8,128)S(1)}, f32[16,1024]{1,0:T(8,128)}, u32[]{:S(2)}) copy-start(f32[16,1024]{1,0:T(8,128)} %param.18) | copy-start | bytes 196612
  525.1 32.1 %copy-start.5 = (f32[128,128]{1,0:T(8,128)}, f32[128,128]{1,0:T(8,128)S(1)}, u32[]{:S(2)}) copy-start(f32[128,128]{1,0:T(8,128)S(1)} %get-tuple-element.18) | copy-start | bytes 196612
Sparse Core Ops, SparseCore 0:
  11.8 89.6 all-reduce.6
  105.8 57.6 all-reduce.8
  167.7 79.9 all-reduce.10
  250.5 29.6 reduce-scatter.6
  284.3 85.8 all-reduce.12
  381.8 57.4 all-reduce.14
  443.4 79.9 all-reduce.16
  525.8 29.6 reduce-scatter.8
where the time goes:
time: 565 us; the launch traced here: 564 us
  waiting for transfers between devices  449 us (79%)
  matrix products  36.6 us (6%)
  other arithmetic  32.3 us (6%)
  blocking collectives  26.5 us (5%)
  between operations  14.4 us (3%)
    psum x4, waiting for transfers between devices, from_root(): return lax.psum(kept, axis)  290 us
    psum x2, waiting for transfers between devices, summed_block(): rows_sum = lax.psum(partial_value, 'row')  98.4 us
    reduce_scatter x1, waiting for transfers between devices, per_device(): lax.psum_scatter(jnp.dot(solved_two.T, trail, preferred_element_type=jnp....  30.7 us
    reduce_scatter x1, waiting for transfers between devices, per_device(): lax.psum_scatter((jnp.dot(head_rows.T, row_two, preferred_element_type=jn...  30.3 us
    another operation x2, other arithmetic, inverse_lower(): return lax.linalg.triangular_solve(block, ident, left_side=True, lower=True)  19.6 us
    all_gather x1, blocking collectives, per_device(): lax.all_gather(row_two, 'row', axis=0, tiled=True)  13.5 us
    all_gather x1, blocking collectives, per_device(): lax.all_gather(row_one, 'row', axis=0, tiled=True)  13 us
  transfers between devices with their start and end apart: 8, of which 8 were waited for; matrix products, arithmetic and copies ran while one was open for 9% of the time, Pallas kernels for 0%

commit v1 on v0

--- a/solution.py
+++ b/solution.py
@@ -6,9 +6,14 @@
 exact_mode = lax.Precision.HIGHEST
 
 
+def refer_the_loops(frame_in, dev_axis):
+    current_block = lax.all_gather(frame_in, axis_name=dev_axis)
+    return jnp.sum(current_block, 0)
+
+
 def from_root(value, axis, source):
     kept = jnp.where(lax.axis_index(axis) == source, value, 0).astype(value.dtype)
-    return lax.psum(kept, axis)
+    return refer_the_loops(kept, axis)
 
 
 def halved_lower(matrix):

time: 565 us -> 538 us (0.952)
  waiting for transfers between devices: 449 us -> 415 us
  other arithmetic: 32.3 us -> 48.3 us
  matrix products: 36.6 us -> 25 us
    psum x4 -> x0, waiting for transfers between devices: 290 us -> none  [from_root(): return lax.psum(kept, axis)]
    all_gather x0 -> x4, waiting for transfers between devices: none -> 239 us  [refer_the_loops(): current_block = lax.all_gather(frame_in, axis_name=dev_axis)]
    psum x2, waiting for transfers between devices: 98.4 us -> 116 us  [summed_block(): rows_sum = lax.psum(partial_value, 'row')]
    unnamed x0 -> x2, other arithmetic: none -> 13.4 us
where the time goes in v1:
time: 538 us
  waiting for transfers between devices  415 us (77%)
  other arithmetic  48.3 us (9%)
  blocking collectives  25.9 us (5%)
  matrix products  25 us (5%)
  between operations  14.4 us (3%)
  local copies, waits for them, and re-layouts  8.28 us (2%)
    all_gather x4, waiting for transfers between devices, refer_the_loops(): current_block = lax.all_gather(frame_in, axis_name=dev_axis)  239 us
    psum x2, waiting for transfers between devices, summed_block(): rows_sum = lax.psum(partial_value, 'row')  116 us
    reduce_scatter x1, waiting for transfers between devices, per_device(): lax.psum_scatter(jnp.dot(solved_two.T, trail, preferred_element_type=jnp....  30.4 us
    reduce_scatter x1, waiting for transfers between devices, per_device(): lax.psum_scatter((jnp.dot(head_rows.T, row_two, preferred_element_type=jn...  30 us
    another operation x2, other arithmetic, inverse_lower(): return lax.linalg.triangular_solve(block, ident, left_side=True, lower=True)  19.6 us
    unnamed x2, other arithmetic  13.4 us
    all_gather x1, blocking collectives, per_device(): lax.all_gather(row_one, 'row', axis=0, tiled=True)  13 us
    all_gather x1, blocking collectives, per_device(): lax.all_gather(row_two, 'row', axis=0, tiled=True)  12.8 us
  transfers between devices with their start and end apart: 8, of which 8 were waited for; matrix products, arithmetic and copies ran while one was open for 9% of the time, Pallas kernels for 0%

profile of v1, /device:TPU:0, one launch (start us, length us, event | category | flops | bytes accessed | tf_op | source)
XLA Modules:
  0.0 537.7 jit_solution(13866430416754330291)
XLA Ops:
  7.2 2.3 slice_select_fusion.1
  10.4 9.8 %custom-call.4 = f32[1,128,128]{1,2,0:T(8,128)S(1)} custom-call(f32[1,128,128]{2,1,0:T(8,128)S(1)} %select_bitcast_fusion.1), custom_call_target="InvertDiagBlocksLowerTriangular" | custom-call | tf_op jit(solution)/shard_map/triangular_solve/custom-call.1 | solution.py:29
  20.5 104.2 %all-gather.10.cloned.1.call-done = f32[32768,128]{1,0:T(8,128)} async-done(((f32[2048,128]{1,0:T(8,128)}), f32[32768,128]{1,0:T(8,128)}) %all-gather.10.cloned.1.call-update) | async-done | bytes 16777232 | tf_op jit(solution)/shard_map/all_gather | solution.py:10
  124.7 6.6 %reduce_sum.36 = f32[2048,128]{1,0:T(8,128)S(1)} reduce(f32[16,2048,128]{2,1,0:T(8,128)} %bitcast.54, f32[]{:T(128)} %constant.29.clone.1), dimensions={0}, to_apply=%region_0.1 | reduce | flops 3932160 | bytes 17825796
  131.4 1.0 convolution_convert_fusion.1
  132.4 2.0 fusion.6
  134.5 58.3 %all-reduce.3.cloned.1.call-done = f32[128,128]{1,0:T(8,128)} async-done(((f32[128,128]{1,0:T(8,128)}), f32[128,128]{1,0:T(8,128)}) %all-reduce.3.cloned.1.call-update) | async-done | bytes 65552 | tf_op jit(solution)/shard_map/psum | solution.py:72
  193.5 12.8 %all_gather.30 = bf16[128,1024]{1,0:T(8,128)(2,1)S(1)} all-gather(bf16[16,1024]{1,0:T(8,128)(2,1)S(1)} %copy-done.5), channel_id=1, replica_groups=mesh['row'=8,'col'=16] {'row'}, dimensions={0}, use_global_device_ids=true | all-gather | bytes 294912 | tf_op jit(solution)/shard_map/all_gather | solution.py:61
  206.3 3.6 convolution_convert_fusion.2
  210.0 4.7 convolution_subtract_fusion.1
  214.6 3.2 copy-done
  218.1 19.5 %all-gather.12.cloned.1.call-done = f32[2048,128]{1,0:T(8,128)} async-done(((f32[128,128]{1,0:T(8,128)}), f32[2048,128]{1,0:T(8,128)}) %all-gather.12.cloned.1.call-update) | async-done | bytes 1048592 | tf_op jit(solution)/shard_map/all_gather | solution.py:10
  237.6 1.3 reduce_sum.37
  239.8 30.4 %reduce-scatter.7.cloned.1.call-done = bf16[16,1024]{1,0:T(8,128)(2,1)} async-done(((bf16[128,1024]{1,0:T(8,128)(2,1)}), bf16[16,1024]{1,0:T(8,128)(2,1)}) %reduce-scatter.7.cloned.1.call-update) | async-done | bytes 32784 | tf_op jit(solution)/shard_map/reduce_scatter | solution.py:83
  270.2 1.0 convolution_subtract_fusion.4
  271.2 1.0 maximum_select_fusion
  272.4 9.8 %custom-call.5 = f32[1,128,128]{1,2,0:T(8,128)S(1)} custom-call(f32[1,128,128]{2,1,0:T(8,128)S(1)} %select_bitcast_fusion), custom_call_target="InvertDiagBlocksLowerTriangular" | custom-call | tf_op jit(solution)/shard_map/triangular_solve/custom-call.1 | solution.py:29
  282.2 13.0 %all_gather.34 = bf16[128,1024]{1,0:T(8,128)(2,1)S(1)} all-gather(bf16[16,1024]{1,0:T(8,128)(2,1)S(1)} %copy-done.12), channel_id=1, replica_groups=mesh['row'=8,'col'=16] {'row'}, dimensions={0}, use_global_device_ids=true | all-gather | bytes 294912 | tf_op jit(solution)/shard_map/all_gather | solution.py:60
  295.5 88.4 %all-gather.8.cloned.1.call-done = f32[16,2064,128]{2,1,0:T(8,128)} async-done(((f32[1,2064,128]{2,1,0:T(8,128)}), f32[16,2064,128]{2,1,0:T(8,128)}) %all-gather.8.cloned.1.call-update) | async-done | bytes 16908304 | tf_op jit(solution)/shard_map/all_gather | solution.py:10
  383.9 6.7 %reduce_sum.38 = f32[2064,128]{1,0:T(8,128)S(1)} reduce(f32[16,2064,128]{2,1,0:T(8,128)} %all-gather.8.cloned.1.call-done, f32[]{:T(128)} %constant.29.clone.1), dimensions={0}, to_apply=%region_4.6 | reduce | flops 3962880 | bytes 17965060
  390.6 1.0 convolution_convert_fusion
  391.8 2.0 convolution_add_fusion.1
  394.0 58.1 %all-reduce.5.cloned.1.call-done = f32[128,128]{1,0:T(8,128)} async-done(((f32[128,128]{1,0:T(8,128)}), f32[128,128]{1,0:T(8,128)}) %all-reduce.5.cloned.1.call-update) | async-done | bytes 65552 | tf_op jit(solution)/shard_map/psum | solution.py:72
  452.9 4.6 convolution_subtract_fusion
  457.5 2.0 copy-done.2
  459.5 2.3 slice.99
  463.0 1.5 fusion
  464.5 1.2 fusion.4
  465.8 4.7 pad_maximum_fusion
  470.5 26.5 %all-gather.14.cloned.1.call-done = f32[2048,128]{1,0:T(8,128)} async-done(((f32[128,128]{1,0:T(8,128)}), f32[2048,128]{1,0:T(8,128)}) %all-gather.14.cloned.1.call-update) | async-done | bytes 1048592 | tf_op jit(solution)/shard_map/all_gather | solution.py:10
  497.0 1.3 reduce_sum.39
  499.2 30.0 %reduce-scatter.9.cloned.1.call-done = bf16[16,1024]{1,0:T(8,128)(2,1)} async-done(((bf16[128,1024]{1,0:T(8,128)(2,1)}), bf16[16,1024]{1,0:T(8,128)(2,1)}) %reduce-scatter.9.cloned.1.call-update) | async-done | bytes 32784 | tf_op jit(solution)/shard_map/reduce_scatter | solution.py:105
  (67 shorter events, 8.3 us)
Async XLA Ops:
  7.2 117.6 %all-gather.10.cloned.1.call-start = ((), (), s32[]{:S(2)}) async-start(), calls=%async_computation.5 | async-start | bytes 17825792 | tf_op jit(solution)/shard_map/all_gather | solution.py:10
  9.5 183.2 %all-reduce.3.cloned.1.call-start = ((), (), s32[]{:S(2)}) async-start(), calls=%async_computation.2 | async-start | bytes 131072 | tf_op jit(solution)/shard_map/psum | solution.py:72
  124.7 68.7 %copy-start.5 = (bf16[16,1024]{1,0:T(8,128)(2,1)S(1)}, bf16[16,1024]{1,0:T(8,128)(2,1)}, u32[]{:S(2)}) copy-start(bf16[16,1024]{1,0:T(8,128)(2,1)} %param.14) | copy-start | bytes 98308
  134.4 103.2 %all-gather.12.cloned.1.call-start = ((), (), s32[]{:S(2)}) async-start(), calls=%async_computation.6 | async-start | bytes 1114112 | tf_op jit(solution)/shard_map/all_gather | solution.py:10
  193.4 76.8 %reduce-scatter.7.cloned.1.call-start = ((), (), s32[]{:S(2)}) async-start(), calls=%async_computation.8 | async-start | bytes 294912 | tf_op jit(solution)/shard_map/reduce_scatter | solution.py:83
  210.0 28.9 %copy-start.3 = (f32[128,128]{1,0:T(8,128)S(1)}, f32[128,128]{1,0:T(8,128)}, u32[]{:S(2)}) copy-start(f32[128,128]{1,0:T(8,128)} %param.16) | copy-start | bytes 196612
  210.0 28.9 %copy-start.8 = (f32[128,128]{1,0:T(8,128)S(1)}, f32[128,128]{1,0:T(8,128)}, u32[]{:S(2)}) copy-start(f32[128,128]{1,0:T(8,128)} %param.21) | copy-start | bytes 196612
  214.6 3.3 copy-start
  217.9 52.4 %copy-start.9 = (f32[16,1024]{1,0:T(8,128)S(1)}, f32[16,1024]{1,0:T(8,128)}, u32[]{:S(2)}) copy-start(f32[16,1024]{1,0:T(8,128)} %param.19) | copy-start | bytes 196612
  217.9 54.5 %copy-start.4 = (f32[128,128]{1,0:T(8,128)S(1)}, f32[128,128]{1,0:T(8,128)}, u32[]{:S(2)}) copy-start(f32[128,128]{1,0:T(8,128)} %param.15) | copy-start | bytes 196612
  217.9 64.3 %copy-start.12 = (bf16[16,1024]{1,0:T(8,128)(2,1)S(1)}, bf16[16,1024]{1,0:T(8,128)(2,1)}, u32[]{:S(2)}) copy-start(bf16[16,1024]{1,0:T(8,128)(2,1)} %param.13) | copy-start | bytes 98308
  218.1 165.8 %all-gather.8.cloned.1.call-start = ((), (), s32[]{:S(2)}) async-start(), calls=%async_computation.3 | async-start | bytes 17965056 | tf_op jit(solution)/shard_map/all_gather | solution.py:10
  239.7 150.9 %copy-start.6 = (f32[128,128]{1,0:T(8,128)}, f32[128,128]{1,0:T(8,128)S(1)}, u32[]{:S(2)}) copy-start(f32[128,128]{1,0:T(8,128)S(1)} %get-tuple-element.16) | copy-start | bytes 196612
  272.3 179.9 %all-reduce.5.cloned.1.call-start = ((), (), s32[]{:S(2)}) async-start(), calls=%async_computation.4 | async-start | bytes 131072 | tf_op jit(solution)/shard_map/psum | solution.py:72
  393.8 103.2 %all-gather.14.cloned.1.call-start = ((), (), s32[]{:S(2)}) async-start(), calls=%async_computation.7 | async-start | bytes 1114112 | tf_op jit(solution)/shard_map/all_gather | solution.py:10
  452.8 76.4 %reduce-scatter.9.cloned.1.call-start = ((), (), s32[]{:S(2)}) async-start(), calls=%async_computation.9 | async-start | bytes 294912 | tf_op jit(solution)/shard_map/reduce_scatter | solution.py:105
  457.5 2.0 copy-start.2
  459.5 3.5 copy-start.1
  465.8 32.5 %copy-start.10 = (f32[128,128]{1,0:T(8,128)S(1)}, f32[128,128]{1,0:T(8,128)}, u32[]{:S(2)}) copy-start(f32[128,128]{1,0:T(8,128)} %param.20) | copy-start | bytes 196612
  465.8 63.4 %copy-start.11 = (f32[16,1024]{1,0:T(8,128)S(1)}, f32[16,1024]{1,0:T(8,128)}, u32[]{:S(2)}) copy-start(f32[16,1024]{1,0:T(8,128)} %param.18) | copy-start | bytes 196612
  499.1 31.7 %copy-start.7 = (f32[128,128]{1,0:T(8,128)}, f32[128,128]{1,0:T(8,128)S(1)}, u32[]{:S(2)}) copy-start(f32[128,128]{1,0:T(8,128)S(1)} %get-tuple-element.18) | copy-start | bytes 196612
Sparse Core Ops, SparseCore 0:
  10.7 113.9 all-gather.9
  134.5 58.1 all-reduce.2
  195.7 41.8 all-gather.11
  240.5 29.6 reduce-scatter.6
  272.8 111.0 all-gather.7
  394.0 58.1 all-reduce.4
  455.1 41.8 all-gather.13
  499.5 29.6 reduce-scatter.8
